TPU v7x, 32 devices: a whole 2x2x4 slice. The times are simulated.
32 devices in a mesh: seq: 8 (over z, x), fsdp: 4 (over y, core).
Axes of the slice: x: 2, y: 2, z: 4, core: 2. Of those that a mesh axis runs over, the one named last changes fastest.
Arguments:
- tokens: bfloat16 [4, 2048, 1536], P('fsdp', 'seq'), may hold values from -6 to 6
- lengths: int32 [4], P('fsdp'), may hold values from 512 to 2048, as said below
- norm_gain: bfloat16 [1536], P('fsdp'), may hold values from 0.099609375 to 1.8984375
- in_weight: bfloat16 [1536, 6448], P('fsdp'), may hold values from -0.15625 to 0.15625
- conv_weight: bfloat16 [4, 3328], P(None, 'fsdp'), may hold values from -3 to 3
- conv_bias: bfloat16 [3328], P('fsdp'), may hold values from -0.5 to 0.5
- dt_bias: bfloat16 [48], P('fsdp'), may hold values from -4.5 to -3.5
- decay_log: bfloat16 [48], P('fsdp'), may hold values from -9 to 0
- skip_gain: bfloat16 [48], P('fsdp'), may hold values from 0.5 to 1.5
- gated_gain: bfloat16 [3072], P('fsdp'), may hold values from 0.099609375 to 1.8984375
- out_weight: bfloat16 [3072, 1536], P('fsdp'), may hold values from -0.109375 to 0.109375
- cotangent: bfloat16 [4, 2048, 1536], P('fsdp', 'seq'), may hold values from -6 to 6
Outputs:
- mixed: bfloat16 [4, 2048, 1536], P('fsdp', 'seq')
- input_grad: float32 [4, 2048, 1536], P('fsdp', 'seq')
- norm_gain_grad: float32 [1536], P('fsdp')
- in_weight_grad: float32 [1536, 6448], P('fsdp')
- conv_weight_grad: float32 [4, 3328], P(None, 'fsdp')
- conv_bias_grad: float32 [3328], P('fsdp')
- dt_bias_grad: float32 [48], P('fsdp')
- decay_log_grad: float32 [48], P('fsdp')
- skip_gain_grad: float32 [48], P('fsdp')
- gated_gain_grad: float32 [3072], P('fsdp')
- out_weight_grad: float32 [3072, 1536], P('fsdp')
Inputs may be any that keep to these rules, and one draw needn't show every extreme that they name: `lengths`: each slot's valid positions come first; some slot has all 2048 valid.
All inputs are finite; a program needn't handle non-finite values.
Results may differ from a plain program's by a relative error of at most 0.012.
The roundings to bfloat16 on the way count: a program that leaves them out, or rounds other values in their place, can miss the bound.
Values may be sent and summed in bfloat16 or wider, within the bound.
No kernel may reach another device: no remote copies, remote signals or barrier semaphores. Data moves between devices by JAX's collectives and lax.ppermute only.
A program may use at most 256 MiB of HBM per device.

v0:
```python
import jax
import jax.numpy as jnp
from jax import lax
from jax.sharding import PartitionSpec as P

epsilon = 1e-05
triple = lax.Precision.HIGH


def from_behind(value, axis, by):
    count = lax.axis_size(axis)
    pairs = [(i, i + by) for i in range(count) if 0 <= i + by < count]
    return lax.ppermute(value, axis, pairs)


def carried_in(value, axis, combine, identity, reverse):
    count, position = (lax.axis_size(axis), lax.axis_index(axis))
    everything = jax.tree.map(lambda part: lax.all_gather(part, axis), value)
    start = jax.tree.map(
        lambda part, zero: jnp.broadcast_to(jnp.asarray(zero, part.dtype), part.shape),
        value,
        identity,
    )

    def lap(k, before):
        at = count - 1 - k if reverse else k
        reached = at > position if reverse else at < position
        new = combine(before, jax.tree.map(lambda part: part[at], everything))
        return jax.tree.map(lambda a, b: jnp.where(reached, a, b), new, before)

    return lax.fori_loop(0, count, lap, start)


def rms_scale(inputs, gain):
    inv_rms = lax.rsqrt(jnp.mean(inputs * inputs, axis=-1, keepdims=True) + epsilon)
    return inputs * inv_rms * gain


def convolve(extended, conv_w, conv_b):
    taps = conv_w.shape[0]
    count = extended.shape[1] - taps + 1
    summed = conv_b + jnp.zeros(extended[:, :count].shape, jnp.float32)
    for offset in range(taps):
        summed = summed + extended[:, offset : offset + count] * conv_w[offset]
    return jax.nn.silu(summed)


def local_scan(values, b_rows, c_rows, step_raw, dt_b, decay_l):
    step_size = jax.nn.softplus(step_raw + dt_b)
    log_decay = jnp.cumsum(-step_size * jnp.exp(decay_l), axis=1)
    count = values.shape[1]
    places = jnp.arange(count)
    lower = (places[:, None] >= places[None, :])[None, :, :, None]
    gaps = log_decay[:, :, None, :] - log_decay[:, None, :, :]
    weights = jnp.where(lower, jnp.exp(jnp.where(lower, gaps, 0.0)), 0.0)
    intersection = jnp.einsum("stn,sun->stu", c_rows, b_rows, precision=triple)
    mixing = weights * intersection[..., None] * step_size[:, None, :, :]
    local_out = jnp.einsum("stuh,suhp->sthp", mixing, values, precision=triple)
    to_end = jnp.exp(log_decay[:, -1:, :] - log_decay) * step_size
    local_state = jnp.einsum("sqh,sqhp,sqn->shpn", to_end, values, b_rows, precision=triple)
    return (local_out, local_state, jnp.exp(log_decay[:, -1, :]), jnp.exp(log_decay))


def finish(local_out, c_rows, decay_in, state_in, values, skip_g, gate_part, gated_g):
    carried_out = decay_in[..., None] * jnp.einsum(
        "sqn,shpn->sqhp", c_rows, state_in, precision=triple
    )
    mixed_heads = local_out + carried_out + skip_g[:, None] * values
    flat = mixed_heads.reshape(gate_part.shape)
    return rms_scale(flat * jax.nn.silu(gate_part), gated_g)


def chain(earlier, later):
    return (earlier[0] * later[0], later[0][..., None, None] * earlier[1] + later[1])


def per_device(
    tokens,
    lengths,
    norm_gain,
    in_weight,
    conv_weight,
    conv_bias,
    dt_bias,
    decay_log,
    skip_gain,
    gated_gain,
    out_weight,
    cotangent,
):
    gathered = (
        lax.all_gather(norm_gain, "fsdp", axis=0, tiled=True),
        lax.all_gather(in_weight, "fsdp", axis=0, tiled=True),
        lax.all_gather(conv_weight, "fsdp", axis=1, tiled=True),
        lax.all_gather(conv_bias, "fsdp", axis=0, tiled=True),
        lax.all_gather(dt_bias, "fsdp", axis=0, tiled=True),
        lax.all_gather(decay_log, "fsdp", axis=0, tiled=True),
        lax.all_gather(skip_gain, "fsdp", axis=0, tiled=True),
        lax.all_gather(gated_gain, "fsdp", axis=0, tiled=True),
        lax.all_gather(out_weight, "fsdp", axis=0, tiled=True),
    )
    full_in = gathered[1]
    full_out = gathered[8]
    norm_f, conv_wf, conv_bf, dtb_f, decay_f, skip_f, ggain_f = [
        gathered[index].astype(jnp.float32) for index in (0, 2, 3, 4, 5, 6, 7)
    ]
    slots, seg, width = tokens.shape
    inner = full_out.shape[0]
    heads = dtb_f.shape[0]
    head_size = inner // heads
    conv_width = conv_wf.shape[1]
    state_width = (conv_width - inner) // 2
    taps = conv_wf.shape[0]
    places = lax.axis_index("seq") * seg + jnp.arange(seg)
    valid = (places[None, :] < lengths[:, None]).astype(jnp.float32)
    inputs = tokens.astype(jnp.float32)
    normed_f, pull_norm = jax.vjp(rms_scale, inputs, norm_f)
    normed = normed_f.astype(jnp.bfloat16)
    projected = jnp.einsum(
        "sqd,dp->sqp", normed, full_in, preferred_element_type=jnp.float32
    ).astype(jnp.bfloat16)
    gate_part = projected[..., :inner].astype(jnp.float32)
    conv_in = projected[..., inner : inner + conv_width]
    step_raw = projected[..., inner + conv_width :].astype(jnp.float32)
    previous = from_behind(conv_in[:, seg - (taps - 1) :], "seq", 1)
    extended = jnp.concatenate([previous, conv_in], axis=1).astype(jnp.float32)
    activated_f, pull_conv = jax.vjp(convolve, extended, conv_wf, conv_bf)
    activated = lax.optimization_barrier(activated_f.astype(jnp.bfloat16)).astype(jnp.float32)
    values = activated[..., :inner].reshape(slots, seg, heads, head_size)
    b_rows = activated[..., inner : inner + state_width]
    c_rows = activated[..., inner + state_width :]
    scanned, pull_local = jax.vjp(local_scan, values, b_rows, c_rows, step_raw, dtb_f, decay_f)
    local_out, local_state, whole_decay, decay_in = scanned
    identity = (
        jnp.ones((slots, heads), jnp.float32),
        jnp.zeros((slots, heads, head_size, state_width), jnp.float32),
    )
    state_in = carried_in((whole_decay, local_state), "seq", chain, identity, False)[1]
    gated_f, pull_finish = jax.vjp(
        finish, local_out, c_rows, decay_in, state_in, values, skip_f, gate_part, ggain_f
    )
    gated_out = gated_f.astype(jnp.bfloat16)
    branch = jnp.einsum("sqi,id->sqd", gated_out, full_out, preferred_element_type=jnp.float32)
    mixed = (valid[..., None] * (inputs + branch)).astype(jnp.bfloat16)
    back_in, back_out = (
        lax.all_gather(in_weight, "fsdp", axis=0, tiled=True),
        lax.all_gather(out_weight, "fsdp", axis=0, tiled=True),
    )
    upstream = valid[..., None] * cotangent.astype(jnp.float32)
    back_branch = upstream.astype(jnp.bfloat16)
    grad_out_w = jnp.einsum(
        "sqi,sqd->id", gated_out, back_branch, preferred_element_type=jnp.float32
    )
    back_gated = jnp.einsum(
        "sqd,id->sqi", back_branch, back_out, preferred_element_type=jnp.float32
    )
    d_local, d_crows_one, d_decay_in, d_state_local, d_values_one, d_skip, d_gate, d_ggain = (
        pull_finish(back_gated)
    )
    state_after = carried_in((whole_decay, d_state_local), "seq", chain, identity, True)[1]
    d_whole = jnp.sum(state_after * state_in, axis=(2, 3))
    d_values_two, d_brows, d_crows_two, d_step, d_dtb, d_decay = pull_local(
        (d_local, state_after, d_whole, d_decay_in)
    )
    d_active = jnp.concatenate(
        [
            (d_values_one + d_values_two).reshape(slots, seg, inner),
            d_brows,
            d_crows_one + d_crows_two,
        ],
        axis=-1,
    )
    d_extended, d_conv_w, d_conv_b = pull_conv(d_active)
    returned = from_behind(d_extended[:, : taps - 1].astype(jnp.bfloat16), "seq", -1).astype(
        jnp.float32
    )
    d_conv_in = d_extended[:, taps - 1 :] + jnp.pad(returned, ((0, 0), (seg - taps + 1, 0), (0, 0)))
    back_projected = jnp.concatenate([d_gate, d_conv_in, d_step], axis=-1).astype(jnp.bfloat16)
    grad_in_w = jnp.einsum(
        "sqd,sqp->dp", normed, back_projected, preferred_element_type=jnp.float32
    )
    back_normed = jnp.einsum(
        "sqp,dp->sqd", back_projected, back_in, preferred_element_type=jnp.float32
    )
    d_inputs, d_norm = pull_norm(back_normed)
    input_grad = upstream + d_inputs
    shares = (
        lax.psum_scatter(d_norm, "fsdp", scatter_dimension=0, tiled=True),
        lax.psum_scatter(grad_in_w, "fsdp", scatter_dimension=0, tiled=True),
        lax.psum_scatter(d_conv_w, "fsdp", scatter_dimension=1, tiled=True),
        lax.psum_scatter(d_conv_b, "fsdp", scatter_dimension=0, tiled=True),
        lax.psum_scatter(d_dtb, "fsdp", scatter_dimension=0, tiled=True),
        lax.psum_scatter(d_decay, "fsdp", scatter_dimension=0, tiled=True),
        lax.psum_scatter(d_skip, "fsdp", scatter_dimension=0, tiled=True),
        lax.psum_scatter(d_ggain, "fsdp", scatter_dimension=0, tiled=True),
        lax.psum_scatter(grad_out_w, "fsdp", scatter_dimension=0, tiled=True),
    )
    totals = lax.psum(
        (
            shares[0],
            shares[1],
            shares[2],
            shares[3],
            shares[4],
            shares[5],
            shares[6],
            shares[7],
            shares[8],
        ),
        "seq",
    )
    return (
        mixed,
        input_grad,
        totals[0],
        totals[1],
        totals[2],
        totals[3],
        totals[4],
        totals[5],
        totals[6],
        totals[7],
        totals[8],
    )


def solution(mesh):
    placed = (
        P("fsdp", "seq", None),
        P("fsdp"),
        P("fsdp"),
        P("fsdp", None),
        P(None, "fsdp"),
        P("fsdp"),
        P("fsdp"),
        P("fsdp"),
        P("fsdp"),
        P("fsdp"),
        P("fsdp", None),
        P("fsdp", "seq", None),
    )
    return jax.shard_map(
        per_device,
        mesh=mesh,
        in_specs=placed,
        out_specs=(
            P("fsdp", "seq", None),
            P("fsdp", "seq", None),
            P("fsdp"),
            P("fsdp", None),
            P(None, "fsdp"),
            P("fsdp"),
            P("fsdp"),
            P("fsdp"),
            P("fsdp"),
            P("fsdp"),
            P("fsdp", None),
        ),
        check_vma=False,
    )
```

profile of v0, /device:TPU:0, one launch (start us, length us, event | category | flops | bytes accessed | tf_op | source)
XLA Modules:
  0.0 1545.1 jit_solution(13398759697782761256)
XLA Ops:
  8.1 6.2 all-gather.3
  14.4 5.4 all-gather.2
  22.8 7.5 all-reduce.24
  32.0 105.5 %all-gather.10.cloned.1.call-done = bf16[1536,6448]{0,1:T(8,128)(2,1)} async-done(((bf16[384,6448]{0,1:T(8,128)(2,1)}), bf16[1536,6448]{0,1:T(8,128)(2,1)}) %all-gather.10.cloned.1.call-update) | async-done | bytes 19808272 | tf_op jit(solution)/shard_map/all_gather | solution.py:93
  137.4 9.9 fusion.6
  151.5 4.0 collective-permute-start
  161.4 4.2 multiply_convert_fusion
  165.5 2.7 fusion.126
  168.2 2.6 copy.167
  170.8 3.6 fusion.22
  176.4 5.2 all-gather.4
  187.7 2.7 mul.527
  190.4 3.5 copy.180
  193.9 19.2 %all_gather.53 = f32[8,1,48]{2,1,0:T(1,128)} all-gather(f32[1,1,48]{2,1,0:T(1,128)} %get-tuple-element.423), channel_id=1, replica_groups=mesh['seq'=8,'fsdp'=4] {'seq'}, dimensions={0}, use_global_device_ids=true | all-gather | bytes 1728 | tf_op jit(solution)/shard_map/all_gather | solution.py:18
  213.1 3.6 copy.176
  218.5 131.1 %all-gather.14.cloned.1.call-done = f32[384,64,128]{2,1,0:T(8,128)} async-done(((f32[48,64,128]{2,1,0:T(8,128)}), f32[384,64,128]{2,1,0:T(8,128)}) %all-gather.14.cloned.1.call-update) | async-done | bytes 12582928 | tf_op jit(solution)/shard_map/all_gather | solution.py:18
  349.6 36.0 %while.30 = (s32[]{:T(128)}, f32[1,48,64,128]{3,2,1,0:T(8,128)}, s32[]{:T(128)}, f32[8,1,48]{2,1,0:T(1,128)}, f32[8,1,48,64,128]{4,3,2,1,0:T(8,128)}, /*index=5*/s32[]{:T(128)}, s32[]{:T(128)}) while((s32[]{:T(128)}, f32[1,48,64,128]{3,2,1,0:T(8,128)}, s32[]{:T(128)}, f32[8,1,48]{2,1,0:T(1,128)}, f32[8,1,48,64,128]{4,3,2,1,0:T(8,128)}, ...), condition=%wide.region_4.5_spmd.clone, body=%wide.region_3.4_spmd.clone.sunk | while | flops 1572868 | bytes 4719281 | solution.py:31
  350.7 2.8 fusion.142
  354.7 3.7 fusion.142
  359.5 4.0 fusion.142
  364.6 3.3 fusion.142
  369.1 3.3 fusion.142
  373.5 3.3 fusion.142
  377.9 3.3 fusion.142
  382.4 3.3 fusion.142
  385.7 2.6 fusion.54
  388.6 9.6 fusion.34
  398.2 3.5 copy.177
  401.8 5.1 multiply_reduce_fusion.7
  408.0 5.7 all-gather.12.cloned.1.call-done
  413.7 10.0 fusion.35
  423.7 5.9 multiply_reduce_fusion.5
  433.3 3.5 copy.181
  436.8 4.0 fusion.94
  440.9 12.7 fusion.76
  454.0 3.7 copy.179
  457.7 14.9 fusion.8
  474.1 4.2 multiply_reduce_fusion.6
  484.9 5.0 fusion.63
  491.7 125.8 %all-gather.16.cloned.1.call-done = f32[384,64,128]{2,1,0:T(8,128)} async-done(((f32[48,64,128]{2,1,0:T(8,128)}), f32[384,64,128]{2,1,0:T(8,128)}) %all-gather.16.cloned.1.call-update) | async-done | bytes 12582928 | tf_op jit(solution)/shard_map/all_gather | solution.py:18
  617.5 38.9 %while.31 = (s32[]{:T(128)}, f32[1,48,64,128]{3,2,1,0:T(8,128)}, s32[]{:T(128)}, f32[8,1,48]{2,1,0:T(1,128)}, f32[8,1,48,64,128]{4,3,2,1,0:T(8,128)}, /*index=5*/s32[]{:T(128)}, s32[]{:T(128)}, s32[]{:T(128)}, s32[]{:T(128)}) while((s32[]{:T(128)}, f32[1,48,64,128]{3,2,1,0:T(8,128)}, s32[]{:T(128)}, f32[8,1,48]{2,1,0:T(1,128)}, ...), condition=%wide.region_8.9_spmd.clone, body=%wide.region_7.8_spmd.clone.sunk | while | flops 1572872 | bytes 4719343 | solution.py:31
  618.6 2.8 fusion.143
  622.6 4.0 fusion.143
  627.7 4.1 fusion.143
  633.0 4.1 fusion.143
  638.2 4.1 fusion.143
  643.5 3.5 fusion.143
  648.1 3.3 fusion.143
  652.5 3.8 fusion.143
  656.3 5.2 fusion.26
  669.9 3.8 reduce-window.16
  676.4 11.2 fusion.33
  687.6 3.9 copy.190
  691.5 4.7 fusion.69
  696.2 5.5 multiply_reduce_fusion.4
  712.6 18.4 %fusion.61 = f32[1536,6448]{0,1:T(8,128)} fusion(bf16[256,48]{1,0:T(8,128)(2,1)} %bitcast.336, bf16[256,3328]{1,0:T(8,128)(2,1)} %fusion.42, bf16[256,3072]{1,0:T(8,128)(2,1)} %get-tuple-element.412, bf16[1,256,1536]{2,1,0:T(8,128)(2,1)} %param.16, f32[1536]{0:T(1024)S(1)} %reshape.620, f32[256]{0:T(256)S(1)} %fusion.111), kind=kOutput, calls=%fused_computation.114 | convolution fusion | flops 5082390528 | bytes 43711488 | tf_op jit(solution)/shard_map/sqd,sqp->dp/dot_general | solution.py:179
  733.8 23.9 %reduce-scatter.8.cloned.1.call-done = f32[768,1536]{1,0:T(8,128)} async-done(((f32[3072,1536]{1,0:T(8,128)}), f32[768,1536]{1,0:T(8,128)}) %reduce-scatter.8.cloned.1.call-update) | async-done | bytes 4718608 | tf_op jit(solution)/shard_map/reduce_scatter | solution.py:196
  757.6 279.1 %reduce-scatter.6.cloned.1.call-done = f32[384,6448]{0,1:T(8,128)} async-done(((f32[1536,6448]{0,1:T(8,128)}), f32[384,6448]{0,1:T(8,128)}) %reduce-scatter.6.cloned.1.call-update) | async-done | bytes 9904144 | tf_op jit(solution)/shard_map/reduce_scatter | solution.py:189
  1040.0 7.5 fusion.39
  1047.6 10.0 fusion.44
  1057.6 12.3 all-reduce.23
  1073.3 39.6 %all-reduce.21 = (f32[384]{0:T(512)}, f32[4,832]{1,0:T(4,128)}, f32[832]{0:T(1024)}, f32[12]{0:T(128)}, f32[12]{0:T(128)}, /*index=5*/f32[12]{0:T(128)}, f32[768]{0:T(1024)}) all-reduce(f32[384]{0:T(512)S(1)} %dynamic-slice.5, f32[4,832]{1,0:T(4,128)S(1)} %copy.211, ...), channel_id=1, replica_groups=mesh['seq'=8,'fsdp'=4] {'seq'}, use_global_device_ids=true, to_apply=%region_21.22 | all-reduce | flops 5348 | bytes 42784 | tf_op jit(solution)/shard_map/psum | solution.py:198
  1112.9 414.5 %all-reduce.27.cloned.1.call-done = (f32[384,6448]{0,1:T(8,128)}, f32[768,1536]{1,0:T(8,128)}) async-done(((f32[384,6448]{0,1:T(8,128)}, f32[768,1536]{1,0:T(8,128)}), (f32[384,6448]{0,1:T(8,128)}, f32[768,1536]{1,0:T(8,128)})) %all-reduce.27.cloned.1.call-update) | async-done | bytes 14622736 | tf_op jit(solution)/shard_map/psum | solution.py:198
  1527.4 8.5 copy.231
  (254 shorter events, 87.2 us)
Async XLA Ops:
  7.2 12.7 copy-start.52
  7.2 7.2 copy-start.57
  7.2 14.6 copy-start.59
  7.2 14.8 copy-start.60
  7.2 15.1 copy-start.61
  7.2 15.3 copy-start.53
  7.3 24.4 %copy-start.11 = (bf16[1,256,1536]{2,1,0:T(8,128)(2,1)S(1)}, bf16[1,256,1536]{2,1,0:T(8,128)(2,1)}, u32[]{:S(2)}) copy-start(bf16[1,256,1536]{2,1,0:T(8,128)(2,1)} %param.16) | copy-start | bytes 2359300
  7.3 130.2 %all-gather.10.cloned.1.call-start = ((), (), s32[]{:S(2)}) async-start(), calls=%async_computation.3 | async-start | bytes 24760320 | tf_op jit(solution)/shard_map/all_gather | solution.py:93
  8.0 341.6 %all-gather.14.cloned.1.call-start = ((), (), s32[]{:S(2)}) async-start(), calls=%async_computation.7 | async-start | bytes 14155776 | tf_op jit(solution)/shard_map/all_gather | solution.py:18
  30.3 117.0 %copy-start.62 = (bf16[48]{0:T(256)(128)(2,1)}, bf16[48]{0:T(256)(128)(2,1)S(1)}, u32[]{:S(2)}) copy-start(bf16[48]{0:T(256)(128)(2,1)S(1)} %get-tuple-element.398) | copy-start | bytes 292
  30.9 125.8 %copy-start.40 = (f32[48]{0:T(128)}, f32[48]{0:T(128)S(1)}, u32[]{:S(2)}) copy-start(f32[48]{0:T(128)S(1)} %convert_element_type.95) | copy-start | bytes 580
  31.9 115.4 %copy-start.44 = (f32[256]{0:T(256)}, f32[256]{0:T(256)S(1)}, u32[]{:S(2)}) copy-start(f32[256]{0:T(256)S(1)} %fusion.46) | copy-start | bytes 3076
  31.9 115.4 %copy-start.55 = (f32[48]{0:T(128)}, f32[48]{0:T(128)S(1)}, u32[]{:S(2)}) copy-start(f32[48]{0:T(128)S(1)} %convert_exponential_fusion) | copy-start | bytes 580
  147.3 12.2 copy-start.10
  151.5 8.1 collective-permute-start
  156.7 2.8 copy-start.48
  170.8 5.6 copy-start.54
  174.5 239.2 %all-gather.12.cloned.1.call-start = ((), (), s32[]{:S(2)}) async-start(), calls=%async_computation.4 | async-start | bytes 11796480 | tf_op jit(solution)/shard_map/all_gather | solution.py:100
  175.2 442.3 %all-gather.16.cloned.1.call-start = ((), (), s32[]{:S(2)}) async-start(), calls=%async_computation.8 | async-start | bytes 14155776 | tf_op jit(solution)/shard_map/all_gather | solution.py:18
  385.6 3.0 copy-start.19
  385.6 3.0 copy-start.28
  385.7 3.0 copy-start.64
  388.2 10.0 copy-start.8
  413.6 10.0 copy-start.47
  413.6 10.0 copy-start
  413.6 10.0 copy-start.3
  413.6 10.0 copy-start.6
  413.6 10.1 copy-start.38
  423.7 7.6 copy-start.9
  440.9 316.7 %reduce-scatter.8.cloned.1.call-start = ((), (), s32[]{:S(2)}) async-start(), calls=%async_computation.6 | async-start | bytes 23592960 | tf_op jit(solution)/shard_map/reduce_scatter | solution.py:196
  453.7 583.1 %reduce-scatter.6.cloned.1.call-start = ((), (), s32[]{:S(2)}) async-start(), calls=%async_computation.5 | async-start | bytes 49520640 | tf_op jit(solution)/shard_map/reduce_scatter | solution.py:189
  483.0 7.0 copy-start.22
  663.1 3.5 copy-start.17
  663.1 3.5 copy-start.21
  663.1 3.5 copy-start.23
  663.1 3.6 copy-start.24
  663.1 3.6 copy-start.25
  691.5 4.7 copy-start.7
  696.1 5.5 copy-start.29
  696.2 5.5 copy-start.30
  696.2 5.5 copy-start.31
  702.7 3.0 copy-start.51
  702.7 4.5 copy-start.41
  702.7 4.5 copy-start.49
  704.4 6.0 collective-permute-start.1
  731.1 341.0 %reduce-scatter.10.cloned.1.call-start = ((), (), s32[]{:S(2)}) async-start(), calls=%async_computation.9 | async-start | bytes 2129920
  733.7 793.7 %all-reduce.27.cloned.1.call-start = ((), (), s32[]{:S(2)}) async-start(), calls=%async_computation.10 | async-start | bytes 29245440 | tf_op jit(solution)/shard_map/psum | solution.py:198
  1036.7 3.0 copy-start.37
  1036.7 3.1 copy-start.1
  1036.7 3.2 copy-start.39
  1036.7 3.2 copy-start.43
  1039.9 7.6 copy-start.58
  1039.9 7.6 copy-start.63
  1039.9 7.6 copy-start.12
  1039.9 7.6 copy-start.14
  1040.0 7.6 copy-start.15
  1040.0 7.6 copy-start.27
  1047.5 10.1 copy-start.32
  1047.6 10.1 copy-start.42
  1047.6 10.0 copy-start.56
  1047.6 22.8 %copy-start.45 = (f32[256]{0:T(256)S(1)}, f32[256]{0:T(256)}, u32[]{:S(2)}) copy-start(f32[256]{0:T(256)} %copy-done.44) | copy-start | bytes 3076
  1047.6 22.8 %copy-start.13 = (bf16[1,256,1536]{2,1,0:T(8,128)(2,1)S(1)}, bf16[1,256,1536]{2,1,0:T(8,128)(2,1)}, u32[]{:S(2)}) copy-start(bf16[1,256,1536]{2,1,0:T(8,128)(2,1)} %param.16) | copy-start | bytes 2359300
  1047.6 22.8 %copy-start.20 = (bf16[1,256,1536]{2,1,0:T(8,128)(2,1)S(1)}, bf16[1,256,1536]{2,1,0:T(8,128)(2,1)}, u32[]{:S(2)}) copy-start(bf16[1,256,1536]{2,1,0:T(8,128)(2,1)} %param.27) | copy-start | bytes 2359300
  1527.4 8.5 copy-start.18
  (11 other events, 12.7 us)
Sparse Core Ops, SparseCore 0:
  9.7 127.6 all-gather.9
  174.6 174.9 all-gather.13
  351.2 62.4 all-gather.11
  441.0 176.4 all-gather.15
  619.9 137.6 reduce-scatter.7
  760.3 276.4 reduce-scatter.5
  1039.9 29.6 reduce-scatter.9
  1074.5 452.8 all-reduce.26
where the time goes:
time: 1550 us
  waiting for transfers between devices  1090 us (70%)
  matrix products  135 us (9%)
  other arithmetic  113 us (7%)
  blocking collectives  95.4 us (6%)
  local copies, waits for them, and re-layouts  88.4 us (6%)
  between operations  20.1 us (1%)
    psum x1, waiting for transfers between devices, per_device(): lax.psum((shares[0], shares[1], shares[2], shares[3], shares[4], shares[5...  415 us
    reduce_scatter x1, waiting for transfers between devices, per_device(): lax.psum_scatter(grad_in_w, 'fsdp', scatter_dimension=0, tiled=True)  279 us
    all_gather x2, waiting for transfers between devices, carried_in(): everything = jax.tree.map(lambda part: lax.all_gather(part, axis), value)  257 us
    all_gather x1, waiting for transfers between devices, per_device(): lax.all_gather(in_weight, 'fsdp', axis=0, tiled=True)  105 us
    select_n x16, other arithmetic, lap(): return jax.tree.map(lambda a, b: jnp.where(reached, a, b), new, before)  56.7 us
    psum x1, blocking collectives, per_device(): lax.psum((shares[0], shares[1], shares[2], shares[3], shares[4], shares[5...  39.6 us
    dot_general x3, matrix products, local_scan(): local_out = jnp.einsum('stuh,suhp->sthp', mixing, values, precision=triple)  35.7 us
  transfers between devices with their start and end apart: 10, of which 8 were waited for; matrix products, arithmetic and copies ran while one was open for 17% of the time, Pallas kernels for 0%

commit v1 on v0

--- a/solution.py
+++ b/solution.py
@@ -5,6 +5,27 @@
 
 epsilon = 1e-05
 triple = lax.Precision.HIGH
+
+
+def collect(value, axis, dim):
+    size, mine, extent = (lax.axis_size(axis), lax.axis_index(axis), value.shape[dim])
+    right = [(i, (i + 1) % size) for i in range(size)]
+    behind = [(i, (i - 1) % size) for i in range(size)]
+    out = jnp.zeros((*value.shape[:dim], size * extent, *value.shape[dim + 1 :]), value.dtype)
+    out = lax.dynamic_update_slice_in_dim(out, value, mine * extent, axis=dim)
+    from_left = from_right = value
+    halfway = size // 2
+    for lap in range(1, halfway + 1):
+        from_left = lax.ppermute(from_left, axis, right)
+        out = lax.dynamic_update_slice_in_dim(
+            out, from_left, (mine - lap) % size * extent, axis=dim
+        )
+        if lap < size - halfway:
+            from_right = lax.ppermute(from_right, axis, behind)
+            out = lax.dynamic_update_slice_in_dim(
+                out, from_right, (mine + lap) % size * extent, axis=dim
+            )
+    return out
 
 
 def from_behind(value, axis, by):
@@ -90,7 +111,7 @@
 ):
     gathered = (
         lax.all_gather(norm_gain, "fsdp", axis=0, tiled=True),
-        lax.all_gather(in_weight, "fsdp", axis=0, tiled=True),
+        collect(in_weight, "fsdp", 0),
         lax.all_gather(conv_weight, "fsdp", axis=1, tiled=True),
         lax.all_gather(conv_bias, "fsdp", axis=0, tiled=True),
         lax.all_gather(dt_bias, "fsdp", axis=0, tiled=True),

time: 1550 us -> 1770 us (1.14)
  waiting for transfers between devices: 1090 us -> 1200 us
  blocking collectives: 95.4 us -> 146 us
  local copies, waits for them, and re-layouts: 88.4 us -> 118 us
    ppermute x0 -> x3, waiting for transfers between devices: none -> 105 us  [the longest x2 105 us: collect(): from_left = lax.ppermute(from_left, axis, right)]
    all_gather x1, blocking collectives: 6.22 us -> 54.7 us  [per_device(): lax.all_gather(conv_weight, 'fsdp', axis=1, tiled=True)]
    dynamic_update_slice x0 -> x4, local copies, waits for them, and re-layouts: none -> 19 us  [the longest x2 10.6 us: collect(): lax.dynamic_update_slice_in_dim(out, from_left, (mine - lap) % size * ext...]
  transfers between devices with their start and end apart: 10 -> 13, of which waited for: 8 -> 10; matrix products, arithmetic and copies ran while one was open for 17% -> 17% of each run, Pallas kernels for 0% -> 0%
where the time goes in v1:
time: 1770 us; the launch traced here: 1760 us
  waiting for transfers between devices  1200 us (68%)
  blocking collectives  146 us (8%)
  matrix products  137 us (8%)
  local copies, waits for them, and re-layouts  118 us (7%)
  other arithmetic  115 us (6%)
  starting transfers between devices  20.3 us (1%)
  between operations  20.2 us (1%)
    psum x1, waiting for transfers between devices, per_device(): lax.psum((shares[0], shares[1], shares[2], shares[3], shares[4], shares[5...  418 us
    reduce_scatter x1, waiting for transfers between devices, per_device(): lax.psum_scatter(grad_in_w, 'fsdp', scatter_dimension=0, tiled=True)  279 us
    all_gather x2, waiting for transfers between devices, carried_in(): everything = jax.tree.map(lambda part: lax.all_gather(part, axis), value)  248 us
    all_gather x1, waiting for transfers between devices, per_device(): lax.all_gather(in_weight, 'fsdp', axis=0, tiled=True)  116 us
    ppermute x2, waiting for transfers between devices, collect(): from_left = lax.ppermute(from_left, axis, right)  105 us
    select_n x16, other arithmetic, lap(): return jax.tree.map(lambda a, b: jnp.where(reached, a, b), new, before)  56.9 us
    all_gather x1, blocking collectives, per_device(): lax.all_gather(conv_weight, 'fsdp', axis=1, tiled=True)  54.7 us
    psum x1, blocking collectives, per_device(): lax.psum((shares[0], shares[1], shares[2], shares[3], shares[4], shares[5...  39.2 us
  transfers between devices with their start and end apart: 13, of which 10 were waited for; matrix products, arithmetic and copies ran while one was open for 17% of the time, Pallas kernels for 0%

profile of v1, /device:TPU:0, one launch (start us, length us, event | category | flops | bytes accessed | tf_op | source)
XLA Modules:
  0.0 1757.4 jit_solution(6066765341839422583)
XLA Ops:
  9.7 105.0 %collective-permute-done = bf16[384,6448]{0,1:T(8,128)(2,1)} collective-permute-done((bf16[384,6448]{0,1:T(8,128)(2,1)}, bf16[384,6448]{0,1:T(8,128)(2,1)}, u32[]{:S(2)}, u32[]{:S(2)}) %collective-permute-start) | collective-permute-done | bytes 4952096 | tf_op jit(solution)/shard_map/ppermute | solution.py:19
  117.2 54.7 %all-gather.3 = bf16[4,832,4]{1,2,0:T(4,128)(2,1)S(1)} all-gather(bf16[1,832,4]{1,2,0:T(4,128)(2,1)} %bitcast.345), channel_id=1, replica_groups=mesh['seq'=8,'fsdp'=4] {'fsdp'}, dimensions={0}, use_global_device_ids=true | all-gather | bytes 33280 | tf_op jit(solution)/shard_map/all_gather | solution.py:115
  172.8 8.2 all-gather.2
  187.0 7.6 all-reduce.24
  197.6 7.1 broadcast_in_dim.91
  207.6 5.2 constant_dynamic-update-slice_fusion.2
  212.9 5.5 constant_dynamic-update-slice_fusion.1
  218.3 5.4 constant_dynamic-update-slice_fusion
  223.7 9.9 fusion.6
  237.8 3.3 collective-permute-start.3
  247.0 4.2 multiply_convert_fusion
  256.5 3.7 fusion.22
  262.1 5.4 all-gather.4
  276.3 3.5 copy.180
  279.9 19.3 %all_gather.51 = f32[8,1,48]{2,1,0:T(1,128)} all-gather(f32[1,1,48]{2,1,0:T(1,128)} %get-tuple-element.423), channel_id=1, replica_groups=mesh['seq'=8,'fsdp'=4] {'seq'}, dimensions={0}, use_global_device_ids=true | all-gather | bytes 1728 | tf_op jit(solution)/shard_map/all_gather | solution.py:39
  299.2 3.6 copy.176
  304.5 131.0 %all-gather.14.cloned.1.call-done = f32[384,64,128]{2,1,0:T(8,128)} async-done(((f32[48,64,128]{2,1,0:T(8,128)}), f32[384,64,128]{2,1,0:T(8,128)}) %all-gather.14.cloned.1.call-update) | async-done | bytes 12582928 | tf_op jit(solution)/shard_map/all_gather | solution.py:39
  435.6 36.0 %while.30 = (s32[]{:T(128)}, f32[1,48,64,128]{3,2,1,0:T(8,128)}, s32[]{:T(128)}, f32[8,1,48]{2,1,0:T(1,128)}, f32[8,1,48,64,128]{4,3,2,1,0:T(8,128)}, /*index=5*/s32[]{:T(128)}, s32[]{:T(128)}) while((s32[]{:T(128)}, f32[1,48,64,128]{3,2,1,0:T(8,128)}, s32[]{:T(128)}, f32[8,1,48]{2,1,0:T(1,128)}, f32[8,1,48,64,128]{4,3,2,1,0:T(8,128)}, ...), condition=%wide.region_4.5_spmd.clone, body=%wide.region_3.4_spmd.clone.sunk | while | flops 1572868 | bytes 4719281 | solution.py:52
  440.6 3.7 fusion.142
  445.5 4.0 fusion.142
  450.6 3.3 fusion.142
  455.0 3.3 fusion.142
  459.4 3.3 fusion.142
  463.9 3.3 fusion.142
  474.6 9.6 fusion.34
  484.2 3.5 copy.177
  487.7 5.1 multiply_reduce_fusion.7
  493.9 5.6 all-gather.10.cloned.1.call-done
  499.6 10.1 fusion.35
  509.7 5.9 multiply_reduce_fusion.5
  519.3 3.5 copy.181
  522.8 4.0 fusion.94
  526.9 10.4 reduce-scatter.8.cloned.1.call-start
  537.3 11.6 fusion.76
  549.1 3.7 copy.179
  552.8 14.9 fusion.8
  569.2 4.2 multiply_reduce_fusion.6
  580.1 5.0 fusion.63
  586.8 116.7 %all-gather.16.cloned.1.call-done = f32[384,64,128]{2,1,0:T(8,128)} async-done(((f32[48,64,128]{2,1,0:T(8,128)}), f32[384,64,128]{2,1,0:T(8,128)}) %all-gather.16.cloned.1.call-update) | async-done | bytes 12582928 | tf_op jit(solution)/shard_map/all_gather | solution.py:39
  703.5 39.0 %while.31 = (s32[]{:T(128)}, f32[1,48,64,128]{3,2,1,0:T(8,128)}, s32[]{:T(128)}, f32[8,1,48]{2,1,0:T(1,128)}, f32[8,1,48,64,128]{4,3,2,1,0:T(8,128)}, /*index=5*/s32[]{:T(128)}, s32[]{:T(128)}, s32[]{:T(128)}, s32[]{:T(128)}) while((s32[]{:T(128)}, f32[1,48,64,128]{3,2,1,0:T(8,128)}, s32[]{:T(128)}, f32[8,1,48]{2,1,0:T(1,128)}, ...), condition=%wide.region_8.9_spmd.clone, body=%wide.region_7.8_spmd.clone.sunk | while | flops 1572872 | bytes 4719343 | solution.py:52
  708.7 4.0 fusion.143
  713.8 4.2 fusion.143
  719.1 4.1 fusion.143
  724.4 4.1 fusion.143
  729.7 3.5 fusion.143
  734.3 3.3 fusion.143
  738.8 3.7 fusion.143
  742.5 5.2 fusion.26
  756.1 3.8 reduce-window.16
  762.6 11.0 fusion.33
  773.5 3.9 copy.190
  777.4 4.7 fusion.69
  782.1 5.5 multiply_reduce_fusion.4
  798.6 18.5 %fusion.61 = f32[1536,6448]{0,1:T(8,128)} fusion(bf16[256,48]{1,0:T(8,128)(2,1)} %bitcast.338, bf16[256,3328]{1,0:T(8,128)(2,1)} %fusion.42, bf16[256,3072]{1,0:T(8,128)(2,1)} %get-tuple-element.412, bf16[1,256,1536]{2,1,0:T(8,128)(2,1)} %param.16, f32[1536]{0:T(1024)S(1)} %reshape.620, f32[256]{0:T(256)S(1)} %fusion.111), kind=kOutput, calls=%fused_computation.114 | convolution fusion | flops 5082390528 | bytes 43711488 | tf_op jit(solution)/shard_map/sqd,sqp->dp/dot_general | solution.py:200
  819.8 23.8 %reduce-scatter.8.cloned.1.call-done = f32[768,1536]{1,0:T(8,128)} async-done(((f32[3072,1536]{1,0:T(8,128)}), f32[768,1536]{1,0:T(8,128)}) %reduce-scatter.8.cloned.1.call-update) | async-done | bytes 4718608 | tf_op jit(solution)/shard_map/reduce_scatter | solution.py:217
  843.6 279.1 %reduce-scatter.6.cloned.1.call-done = f32[384,6448]{0,1:T(8,128)} async-done(((f32[1536,6448]{0,1:T(8,128)}), f32[384,6448]{0,1:T(8,128)}) %reduce-scatter.6.cloned.1.call-update) | async-done | bytes 9904144 | tf_op jit(solution)/shard_map/reduce_scatter | solution.py:210
  1125.9 7.4 fusion.39
  1133.4 115.7 %all-gather.12.cloned.1.call-done = bf16[1536,6448]{0,1:T(8,128)(2,1)} async-done(((bf16[384,6448]{0,1:T(8,128)(2,1)}), bf16[1536,6448]{0,1:T(8,128)(2,1)}) %all-gather.12.cloned.1.call-update) | async-done | bytes 19808272 | tf_op jit(solution)/shard_map/all_gather | solution.py:167
  1249.1 13.2 fusion.44
  1262.4 11.3 all-reduce.23
  1275.8 5.7 reduce-scatter.10.cloned.1.call-done
  1282.7 39.2 %all-reduce.21 = (f32[384]{0:T(512)}, f32[4,832]{1,0:T(4,128)}, f32[832]{0:T(1024)}, f32[12]{0:T(128)}, f32[12]{0:T(128)}, /*index=5*/f32[12]{0:T(128)}, f32[768]{0:T(1024)}) all-reduce(f32[384]{0:T(512)S(1)} %dynamic-slice.5, f32[4,832]{1,0:T(4,128)S(1)} %copy.211, ...), channel_id=1, replica_groups=mesh['seq'=8,'fsdp'=4] {'seq'}, use_global_device_ids=true, to_apply=%region_21.22 | all-reduce | flops 5348 | bytes 42784 | tf_op jit(solution)/shard_map/psum | solution.py:219
  1321.8 417.6 %all-reduce.27.cloned.1.call-done = (f32[384,6448]{0,1:T(8,128)}, f32[768,1536]{1,0:T(8,128)}) async-done(((f32[384,6448]{0,1:T(8,128)}, f32[768,1536]{1,0:T(8,128)}), (f32[384,6448]{0,1:T(8,128)}, f32[768,1536]{1,0:T(8,128)})) %all-reduce.27.cloned.1.call-update) | async-done | bytes 14622736 | tf_op jit(solution)/shard_map/psum | solution.py:219
  1739.5 8.5 copy.235
  (250 shorter events, 118.9 us)
Async XLA Ops:
  7.2 428.4 %all-gather.14.cloned.1.call-start = ((), (), s32[]{:S(2)}) async-start(), calls=%async_computation.7 | async-start | bytes 14155776 | tf_op jit(solution)/shard_map/all_gather | solution.py:39
  7.2 107.5 %collective-permute-start = (bf16[384,6448]{0,1:T(8,128)(2,1)}, bf16[384,6448]{0,1:T(8,128)(2,1)}, u32[]{:S(2)}, u32[]{:S(2)}) collective-permute-start(bf16[384,6448]{0,1:T(8,128)(2,1)} %param.19), channel_id=1, source_target_pairs={{0,1},{1,2},{2,3},{3,0},{4,5},{5,6},{6,7},{7,4},{8,9},{9,10},{10,1... | collective-permute-start | bytes 14856200 | tf_op jit(solution)/shard_map/ppermute | solution.py:19
  7.7 205.1 %collective-permute-start.1 = (bf16[384,6448]{0,1:T(8,128)(2,1)}, bf16[384,6448]{0,1:T(8,128)(2,1)}, u32[]{:S(2)}, u32[]{:S(2)}) collective-permute-start(bf16[384,6448]{0,1:T(8,128)(2,1)} %param.19), channel_id=1, source_target_pairs={{0,3},{1,0},{2,1},{3,2},{4,7},{5,4},{6,5},{7,6},{8,11},{9,8},{10,9... | collective-permute-start | bytes 14856200 | tf_op jit(solution)/shard_map/ppermute | solution.py:24
  114.7 103.6 %collective-permute-start.2 = (bf16[384,6448]{0,1:T(8,128)(2,1)}, bf16[384,6448]{0,1:T(8,128)(2,1)}, u32[]{:S(2)}, u32[]{:S(2)}) collective-permute-start(bf16[384,6448]{0,1:T(8,128)(2,1)} %collective-permute-done), channel_id=1, source_target_pairs={{0,1},{1,2},{2,3},{3,0},{4,5},{5,6},{6,7},{7,4},{8,9},{9,10},{10,1... | collective-permute-start | bytes 14856200 | tf_op jit(solution)/shard_map/ppermute | solution.py:19
  194.7 10.0 copy-start.52
  195.3 47.1 %copy-start.37 = (f32[48]{0:T(128)}, f32[48]{0:T(128)S(1)}, u32[]{:S(2)}) copy-start(f32[48]{0:T(128)S(1)} %convert_element_type.95) | copy-start | bytes 580
  196.0 8.6 slice-start
  197.5 7.1 copy-start.41
  197.6 36.1 %copy-start.49 = (f32[48]{0:T(128)}, f32[48]{0:T(128)S(1)}, u32[]{:S(2)}) copy-start(f32[48]{0:T(128)S(1)} %convert_exponential_fusion) | copy-start | bytes 580
  197.6 7.1 slice-start.1
  218.3 5.4 copy-start.11
  233.6 11.5 copy-start.10
  237.8 7.4 collective-permute-start.3
  242.3 2.8 copy-start.45
  251.1 2.8 copy-start.5
  256.5 5.7 copy-start.48
  260.1 239.4 %all-gather.10.cloned.1.call-start = ((), (), s32[]{:S(2)}) async-start(), calls=%async_computation.3 | async-start | bytes 11796480 | tf_op jit(solution)/shard_map/all_gather | solution.py:121
  260.9 442.6 %all-gather.16.cloned.1.call-start = ((), (), s32[]{:S(2)}) async-start(), calls=%async_computation.8 | async-start | bytes 14155776 | tf_op jit(solution)/shard_map/all_gather | solution.py:39
  471.6 2.6 copy-start.4
  471.6 3.0 copy-start.16
  471.6 3.0 copy-start.25
  471.6 3.0 copy-start.54
  474.2 10.0 copy-start.8
  499.6 10.1 copy-start.44
  499.6 10.1 copy-start
  499.6 10.1 copy-start.3
  499.6 10.1 copy-start.6
  499.6 10.1 copy-start.35
  509.7 7.6 copy-start.9
  515.6 1.7 copy-start.2
  526.9 316.7 %reduce-scatter.8.cloned.1.call-start = ((), (), s32[]{:S(2)}) async-start(), calls=%async_computation.6 | async-start | bytes 23592960 | tf_op jit(solution)/shard_map/reduce_scatter | solution.py:217
  549.0 573.7 %reduce-scatter.6.cloned.1.call-start = ((), (), s32[]{:S(2)}) async-start(), calls=%async_computation.5 | async-start | bytes 49520640 | tf_op jit(solution)/shard_map/reduce_scatter | solution.py:210
  578.1 7.0 copy-start.19
  749.2 3.5 copy-start.14
  749.2 3.5 copy-start.18
  749.2 3.5 copy-start.20
  749.2 3.6 copy-start.21
  749.2 3.6 copy-start.22
  777.4 4.7 copy-start.7
  782.1 5.5 copy-start.26
  782.1 5.5 copy-start.27
  782.1 5.5 copy-start.28
  788.6 3.0 copy-start.47
  788.6 4.5 copy-start.38
  788.7 4.5 copy-start.46
  790.3 6.0 collective-permute-start.4
  817.1 0.8 copy-start.30
  817.2 431.9 %all-gather.12.cloned.1.call-start = ((), (), s32[]{:S(2)}) async-start(), calls=%async_computation.4 | async-start | bytes 24760320 | tf_op jit(solution)/shard_map/all_gather | solution.py:167
  817.7 463.8 %reduce-scatter.10.cloned.1.call-start = ((), (), s32[]{:S(2)}) async-start(), calls=%async_computation.9 | async-start | bytes 2129920
  819.8 919.7 %all-reduce.27.cloned.1.call-start = ((), (), s32[]{:S(2)}) async-start(), calls=%async_computation.10 | async-start | bytes 29245440 | tf_op jit(solution)/shard_map/psum | solution.py:219
  1122.7 3.0 copy-start.34
  1122.7 3.1 copy-start.1
  1122.7 3.2 copy-start.36
  1122.7 3.2 copy-start.40
  1125.9 7.4 copy-start.51
  1125.9 7.4 copy-start.53
  1125.9 123.2 %copy-start.24 = (bf16[1,256,48]{2,1,0:T(8,128)(2,1)S(1)}, bf16[1,256,48]{2,1,0:T(8,128)(2,1)}, u32[]{:S(2)}) copy-start(bf16[1,256,48]{2,1,0:T(8,128)(2,1)} %get-tuple-element.404) | copy-start | bytes 73732
  1133.3 129.0 %copy-start.29 = (f32[3328]{0:T(1024)S(1)}, f32[3328]{0:T(1024)}, u32[]{:S(2)}) copy-start(f32[3328]{0:T(1024)} %get-tuple-element.355) | copy-start | bytes 39940
  1133.3 129.0 %copy-start.39 = (f32[3072]{0:T(1024)S(1)}, f32[3072]{0:T(1024)}, u32[]{:S(2)}) copy-start(f32[3072]{0:T(1024)} %get-tuple-element.353) | copy-start | bytes 36868
  1133.3 129.0 %copy-start.50 = (f32[48]{0:T(128)S(1)}, f32[48]{0:T(128)}, u32[]{:S(2)}) copy-start(f32[48]{0:T(128)} %get-tuple-element.403) | copy-start | bytes 580
  1133.4 140.7 %copy-start.42 = (f32[256]{0:T(256)S(1)}, f32[256]{0:T(256)}, u32[]{:S(2)}) copy-start(f32[256]{0:T(256)} %copy-done.41) | copy-start | bytes 3076
  1133.4 140.7 %copy-start.12 = (bf16[1,256,1536]{2,1,0:T(8,128)(2,1)S(1)}, bf16[1,256,1536]{2,1,0:T(8,128)(2,1)}, u32[]{:S(2)}) copy-start(bf16[1,256,1536]{2,1,0:T(8,128)(2,1)} %param.16) | copy-start | bytes 2359300
  1133.4 140.7 %copy-start.17 = (bf16[1,256,1536]{2,1,0:T(8,128)(2,1)S(1)}, bf16[1,256,1536]{2,1,0:T(8,128)(2,1)}, u32[]{:S(2)}) copy-start(bf16[1,256,1536]{2,1,0:T(8,128)(2,1)} %param.27) | copy-start | bytes 2359300
  1739.5 8.5 copy-start.15
  (6 other events, 4.0 us)
Sparse Core Ops, SparseCore 0:
  260.3 175.2 all-gather.13
  437.1 62.4 all-gather.9
  527.0 176.4 all-gather.15
  705.9 137.6 reduce-scatter.7
  846.3 276.4 reduce-scatter.5
  1124.2 124.8 all-gather.11
  1252.2 29.2 reduce-scatter.9
  1286.4 453.0 all-reduce.26
